TPU v7x, 256 devices: a whole 4x4x8 slice. The times are simulated.
256 devices in a mesh: seq: 32 (over y, x, core), exp: 8 (over z).
Axes of the slice: x: 4, y: 4, z: 8, core: 2. Of those that a mesh axis runs over, the one named last changes fastest.
Arguments:
- mixer_input: bfloat16 [4096, 8192], P('seq', 'exp'), may hold values from -6 to 6
- gate_input: bfloat16 [4096, 8192], P('seq', 'exp'), may hold values from -6 to 6
- delta_raw: bfloat16 [4096, 8192], P('seq', 'exp'), may hold values from -7 to 16387
- input_coef: bfloat16 [4096, 16], P('seq'), may hold values from 0.19921875 to 1.796875
- output_coef: bfloat16 [4096, 16], P('seq'), may hold values from -3 to 3
- decay_rate: float32 [16, 8192], P(None, 'exp'), may hold values from 4.8828125e-06 to 0.05
- conv_weight: float32 [4, 8192], P(None, 'exp'), may hold values from -3 to 3
- conv_bias: float32 [8192], P('exp'), may hold values from -3 to 3
- skip_gain: float32 [8192], P('exp'), may hold values from 0.5 to 1.5
- out_weight: bfloat16 [8192, 4096], P('exp', 'seq'), may hold values from -0.0625 to 0.0625
- residual: bfloat16 [4096, 4096], P(('seq', 'exp')), may hold values from -6 to 6
- norm_gain: float32 [4096], replicated, may hold values from 0.1 to 1.9
- router_weight: bfloat16 [4096, 8], replicated, may hold values from -0.09375 to 0.09375
- expert_ids: int32 [4096, 2], P(('seq', 'exp')), may hold values from 0 to 7, all different within a row; in each aligned block of 16 rows (0 to 15, 16 to 31, ...) at most 5 rows name the same one
- gate_weight: bfloat16 [8, 4096, 12288], P('exp', None, 'seq'), may hold values from -0.09375 to 0.09375
- up_weight: bfloat16 [8, 4096, 12288], P('exp', None, 'seq'), may hold values from -0.09375 to 0.09375
- down_weight: bfloat16 [8, 12288, 4096], P('exp', 'seq'), may hold values from -0.0546875 to 0.0546875
Outputs:
- mixed: bfloat16 [4096, 8192], P('seq', 'exp')
- final: bfloat16 [4096, 4096], P(('seq', 'exp'))
Inputs may be any that keep to these rules, and one draw needn't show every extreme that they name: `expert_ids`: each row names two different experts. In each aligned block of 16 rows (the rows of one device) no expert is named by more than 5 rows, and in some block one expert is named by exactly 5 rows.
All inputs are finite; a program needn't handle non-finite values.
Results may differ from a plain program's by a relative error of at most 0.015.
Values may be sent and summed in bfloat16 or wider, within the bound.
No kernel may reach another device: no remote copies, remote signals or barrier semaphores. Data moves between devices by JAX's collectives and lax.ppermute only.
A program may use at most 128 MiB of HBM per device.

v0:
```python
import jax
import jax.numpy as jnp
from jax import lax
from jax.sharding import PartitionSpec as P

KCONV = 4


def from_behind(block, axis, distance):
    devices = range(lax.axis_size(axis))
    route = [(i - distance, i) for i in devices if i - distance in devices]
    return lax.ppermute(block, axis, route)


def carried_in(part, axis, combine, identity):
    place = lax.axis_index(axis)
    gathered = jax.tree.map(lambda a: lax.all_gather(a, axis), part)
    state = jax.tree.map(lambda a, e: jnp.zeros_like(a) + jnp.asarray(e, a.dtype), part, identity)

    def one(turn, state):
        return combine(
            state, jax.tree.map(lambda a: lax.dynamic_index_in_dim(a, turn, 0, False), gathered)
        )

    return lax.fori_loop(0, place, one, state)


def sweep(state, delta, convolved, input_rows, output_rows, decay_rate):

    def advance(carry, inputs):
        delta_row, value_row, input_row, output_row = inputs
        retain = jnp.exp(-delta_row[None, :] * decay_rate)
        carry = retain * carry + (1.0 - retain) * input_row[:, None] * value_row[None, :]
        return (carry, jnp.sum(output_row[:, None] * carry, axis=0))

    return lax.scan(advance, state, (delta, convolved, input_rows, output_rows), unroll=8)


def chain(earlier, later):
    return (earlier[0] * later[0], later[0] * earlier[1] + later[1])


def shards(
    mixer_input,
    gate_input,
    delta_raw,
    input_coef,
    output_coef,
    decay_rate,
    conv_weight,
    conv_bias,
    skip_gain,
    out_weight,
    residual,
    norm_gain,
    router_weight,
    expert_ids,
    gate_weight,
    up_weight,
    down_weight,
):
    length = mixer_input.shape[0]
    width = mixer_input.shape[1]
    tail = mixer_input[length - (KCONV - 1) :]
    before = from_behind(tail, "seq", 1)
    padded = jnp.concatenate([before, mixer_input], axis=0).astype(jnp.float32)
    summed = jnp.broadcast_to(conv_bias[None, :], (length, width))
    for offset in range(KCONV):
        summed = summed + conv_weight[offset][None, :] * padded[offset : offset + length]
    convolved = jax.nn.silu(summed)
    delta = jax.nn.softplus(delta_raw.astype(jnp.float32))
    input_rows = input_coef.astype(jnp.float32)
    output_rows = output_coef.astype(jnp.float32)
    zero_state = jnp.zeros(decay_rate.shape, jnp.float32)
    end_state, local_out = sweep(zero_state, delta, convolved, input_rows, output_rows, decay_rate)
    block_decay = jnp.exp(-jnp.sum(delta, axis=0)[None, :] * decay_rate)
    carried_decay, start_state = carried_in(
        (block_decay, end_state), "seq", chain, (jnp.ones_like(block_decay), zero_state)
    )
    last_state, scan_out = sweep(start_state, delta, convolved, input_rows, output_rows, decay_rate)
    mixed = (
        (scan_out + skip_gain[None, :] * convolved) * jax.nn.silu(gate_input.astype(jnp.float32))
    ).astype(jnp.bfloat16)
    rows = residual.shape[0]
    model_width = residual.shape[1]
    full_weight = lax.all_gather(out_weight, "seq", axis=1, tiled=True)
    projected = lax.psum_scatter(
        jnp.dot(mixed, full_weight, preferred_element_type=jnp.float32).astype(jnp.bfloat16),
        "exp",
        scatter_dimension=0,
        tiled=True,
    ).astype(jnp.float32)
    hidden_state = residual.astype(jnp.float32) + projected
    scale = lax.rsqrt(jnp.mean(hidden_state * hidden_state, axis=1, keepdims=True) + 1e-06)
    normed = (hidden_state * scale * norm_gain[None, :]).astype(jnp.bfloat16)
    experts = router_weight.shape[1]
    capacity = 2 * rows // experts + 1
    logits = jnp.dot(normed, router_weight, preferred_element_type=jnp.float32)
    expert_range = jnp.arange(experts, dtype=jnp.int32)
    matches = expert_ids[:, :, None] == expert_range[None, None, :]
    chosen = jnp.sum(jnp.where(matches, logits[:, None, :], 0.0), axis=2)
    first = jax.nn.sigmoid(chosen[:, 0] - chosen[:, 1])
    flat_ids = expert_ids.reshape(-1)
    onehot = (flat_ids[:, None] == expert_range[None, :]).astype(jnp.int32)
    rank = jnp.sum((jnp.cumsum(onehot, axis=0) - onehot) * onehot, axis=1)
    target = flat_ids * capacity + rank
    placing = (jnp.arange(experts * capacity, dtype=jnp.int32)[:, None] == target[None, :]).astype(
        jnp.bfloat16
    )
    repeated = jnp.broadcast_to(normed[:, None, :], (rows, 2, model_width)).reshape(-1, model_width)
    outgoing = (
        jnp.dot(placing, repeated, preferred_element_type=jnp.float32)
        .astype(jnp.bfloat16)
        .reshape(experts, capacity, model_width)
    )
    arrived = lax.all_to_all(outgoing, "exp", split_axis=0, concat_axis=0, tiled=True)
    flat_rows = arrived.reshape(-1, arrived.shape[2])
    piece = lax.all_gather(flat_rows, "seq", axis=0, tiled=True)
    gating = jnp.dot(piece, gate_weight[0], preferred_element_type=jnp.float32)
    upward = jnp.dot(piece, up_weight[0], preferred_element_type=jnp.float32)
    activated = (jax.nn.silu(gating) * upward).astype(jnp.bfloat16)
    partial_out = jnp.dot(activated, down_weight[0], preferred_element_type=jnp.float32)
    summed_out = lax.psum_scatter(
        partial_out.astype(jnp.bfloat16), "seq", scatter_dimension=0, tiled=True
    )
    returned = lax.all_to_all(
        summed_out.reshape(arrived.shape), "exp", split_axis=0, concat_axis=0, tiled=True
    )
    flat_returned = returned.reshape(-1, model_width)
    picked = jnp.einsum(
        "sa,sd->ad", placing, flat_returned, preferred_element_type=jnp.float32
    ).reshape(rows, 2, model_width)
    moe_out = first[:, None] * picked[:, 0] + (1.0 - first)[:, None] * picked[:, 1]
    final = (hidden_state + moe_out).astype(jnp.bfloat16)
    return (mixed, final)


def solution(mesh):
    return jax.shard_map(
        shards,
        mesh=mesh,
        in_specs=(
            P("seq", "exp"),
            P("seq", "exp"),
            P("seq", "exp"),
            P("seq", None),
            P("seq", None),
            P(None, "exp"),
            P(None, "exp"),
            P("exp"),
            P("exp"),
            P("exp", "seq"),
            P(("seq", "exp"), None),
            P(),
            P(),
            P(("seq", "exp"), None),
            P("exp", None, "seq"),
            P("exp", None, "seq"),
            P("exp", "seq", None),
        ),
        out_specs=(P("seq", "exp"), P(("seq", "exp"), None)),
        check_vma=False,
    )
```

profile of v0, /device:TPU:2, one launch (start us, length us, event | category | flops | bytes accessed | tf_op | source)
XLA Modules:
  0.0 490.1 jit_solution(7569274445757107317)
XLA Ops:
  8.1 2.0 collective-permute-start
  10.2 2.1 fusion.59
  12.2 1.5 multiply_exponential_fusion
  13.8 0.9 fusion.71
  15.5 1.0 maximum_convert_fusion
  17.4 1.8 fusion.81
  19.2 28.9 %while.37 = (s32[]{:T(128)}, f32[16,1024]{1,0:T(8,128)S(1)}, f32[16,8,1024]{2,1,0:T(8,128)}, f32[16,1024]{1,0:T(8,128)S(1)}, f32[16,8,16]{2,1,0:T(8,128)S(1)}, /...) while((s32[]{:T(128)}, f32[16,1024]{1,0:T(8,128)S(1)}, ...), condition=%wide.region_2.3_spmd.clone, body=%wide.region_1.2_spmd.clone.sunk | while | flops 811018 | bytes 396055 | solution.py:36
  19.2 1.4 constant_dynamic-slice_fusion.41
  20.8 1.6 constant_dynamic-slice_fusion.41
  22.6 1.6 constant_dynamic-slice_fusion.41
  24.4 1.5 constant_dynamic-slice_fusion.41
  26.1 1.6 constant_dynamic-slice_fusion.41
  27.9 1.9 constant_dynamic-slice_fusion.41
  30.0 1.6 constant_dynamic-slice_fusion.41
  31.9 1.5 constant_dynamic-slice_fusion.41
  33.7 1.4 constant_dynamic-slice_fusion.41
  35.3 1.5 constant_dynamic-slice_fusion.41
  37.0 1.9 constant_dynamic-slice_fusion.41
  39.1 1.6 constant_dynamic-slice_fusion.41
  40.9 1.6 constant_dynamic-slice_fusion.41
  42.8 1.6 constant_dynamic-slice_fusion.41
  44.6 1.6 constant_dynamic-slice_fusion.41
  46.4 1.6 constant_dynamic-slice_fusion.41
  49.7 16.5 %all-gather.11.cloned.1.call-done = f32[512,1024]{1,0:T(8,128)} async-done(((f32[16,1024]{1,0:T(8,128)}), f32[512,1024]{1,0:T(8,128)}) %all-gather.11.cloned.1.call-update) | async-done | bytes 2097168 | tf_op jit(solution)/shard_map/all_gather | solution.py:17
  66.2 51.3 %all-gather.13.cloned.1.call-done = f32[512,1024]{1,0:T(8,128)} async-done(((f32[16,1024]{1,0:T(8,128)}), f32[512,1024]{1,0:T(8,128)}) %all-gather.13.cloned.1.call-update) | async-done | bytes 2097168 | tf_op jit(solution)/shard_map/all_gather | solution.py:17
  117.5 1.8 while.35
  117.5 0.9 bitcast_add_fusion.3
  118.4 0.9 bitcast_add_fusion.3
  119.4 44.5 %while.36 = (s32[]{:T(128)}, f32[16,1024]{1,0:T(8,128)S(1)}, f32[16,8,1024]{2,1,0:T(8,128)}, f32[16,8,1024]{2,1,0:T(8,128)}, f32[16,1024]{1,0:T(8,128)S(1)}, /*i...) while((s32[]{:T(128)}, f32[16,1024]{1,0:T(8,128)S(1)}, ...), condition=%wide.region_14.15_spmd, body=%wide.region_5.14_spmd.sunk | while | flops 1441801 | bytes 1316385 | solution.py:36
  119.4 1.4 constant_dynamic-slice_fusion.40
  122.0 1.6 constant_dynamic-slice_fusion.40
  124.8 1.6 constant_dynamic-slice_fusion.40
  127.5 1.5 constant_dynamic-slice_fusion.40
  130.2 1.6 constant_dynamic-slice_fusion.40
  133.0 1.9 constant_dynamic-slice_fusion.40
  136.1 1.6 constant_dynamic-slice_fusion.40
  138.9 1.5 constant_dynamic-slice_fusion.40
  141.6 1.4 constant_dynamic-slice_fusion.40
  144.2 1.5 constant_dynamic-slice_fusion.40
  146.9 1.9 constant_dynamic-slice_fusion.40
  150.0 1.6 constant_dynamic-slice_fusion.40
  152.8 1.6 constant_dynamic-slice_fusion.40
  155.6 1.6 constant_dynamic-slice_fusion.40
  158.3 1.6 constant_dynamic-slice_fusion.40
  161.1 1.6 constant_dynamic-slice_fusion.40
  163.8 2.5 fusion.58
  166.4 17.6 %all-gather.7.cloned.1.call-done = bf16[1024,4096]{1,0:T(8,128)(2,1)} async-done(((bf16[1024,128]{1,0:T(8,128)(2,1)}), bf16[1024,4096]{1,0:T(8,128)(2,1)}) %all-gather.7.cloned.1.call-update) | async-done | bytes 8388624 | tf_op jit(solution)/shard_map/all_gather | solution.py:86
  184.0 5.7 %convolution_convert_fusion.1 = bf16[128,4096]{1,0:T(8,128)(2,1)} fusion(bf16[128,1024]{1,0:T(8,128)(2,1)S(1)} %fusion.58, bf16[1024,4096]{1,0:T(8,128)(2,1)} %all-gather.7.cloned.1.call-done), kind=kOutput, calls=%fused_computation.111 | convolution fusion | flops 1074266112 | bytes 9699328 | tf_op jit(solution)/shard_map/dot_general | solution.py:88
  191.5 45.4 %reduce-scatter.3.cloned.1.call-done = bf16[16,4096]{1,0:T(8,128)(2,1)} async-done(((bf16[128,4096]{1,0:T(8,128)(2,1)}), bf16[16,4096]{1,0:T(8,128)(2,1)}) %reduce-scatter.3.cloned.1.call-update) | async-done | bytes 131088 | tf_op jit(solution)/shard_map/reduce_scatter | solution.py:87
  236.9 1.1 multiply_reduce_fusion.8
  238.0 1.0 multiply_convert_fusion
  240.7 1.2 convolution_convert_fusion.2
  241.8 0.9 reshape.356
  242.8 17.9 %all_to_all.10 = bf16[8,5,4096]{2,1,0:T(8,128)(2,1)} all-to-all(bf16[8,5,4096]{2,1,0:T(8,128)(2,1)} %reshape.356), channel_id=1, replica_groups=mesh['seq'=32,'exp'=8] {'exp'}, dimensions={0} | all-to-all | bytes 655360 | tf_op jit(solution)/shard_map/all_to_all | solution.py:116
  260.7 1.9 reshape.357
  262.6 59.5 %all-gather.9.cloned.1.call-done = bf16[1280,4096]{1,0:T(8,128)(2,1)} async-done(((bf16[40,4096]{1,0:T(8,128)(2,1)}), bf16[1280,4096]{1,0:T(8,128)(2,1)}) %all-gather.9.cloned.1.call-update) | async-done | bytes 10485776 | tf_op jit(solution)/shard_map/all_gather | solution.py:118
  322.2 10.2 %fusion.33 = f32[1280,384]{1,0:T(8,128)} fusion(bf16[1280,4096]{1,0:T(8,128)(2,1)} %all-gather.9.cloned.1.call-done, bf16[1,4096,384]{2,1,0:T(8,128)(2,1)} %param.37), kind=kOutput, calls=%fused_computation.116 | convolution fusion | flops 4026531840 | bytes 15597568 | tf_op jit(solution)/shard_map/dot_general | solution.py:119
  332.3 17.2 %convolution_convert_fusion = bf16[1280,4096]{1,0:T(8,128)(2,1)} fusion(bf16[1,384,4096]{2,1,0:T(8,128)(2,1)S(1)} %copy-done, bf16[1280,4096]{1,0:T(8,128)(2,1)} %all-gather.9.cloned.1.call-done, bf16[1,4096,384]{2,1,0:T(8,128)(2,1)} %param.38, f32[1280,384]{1,0:T(8,128)} %fusion.33), kind=kOutput, calls=%fused_computation.110 | convolution fusion | flops 8061255680 | bytes 29229056 | tf_op jit(solution)/shard_map/dot_general | solution.py:122
  349.6 105.2 %reduce-scatter.5.cloned.1.call-done = bf16[40,4096]{1,0:T(8,128)(2,1)} async-done(((bf16[1280,4096]{1,0:T(8,128)(2,1)}), bf16[40,4096]{1,0:T(8,128)(2,1)}) %reduce-scatter.5.cloned.1.call-update) | async-done | bytes 327696 | tf_op jit(solution)/shard_map/reduce_scatter | solution.py:123
  454.8 1.9 reshape.358
  456.7 7.0 %all-to-all-start.1 = ((bf16[8,5,4096]{2,1,0:T(8,128)(2,1)}), bf16[8,5,4096]{2,1,0:T(8,128)(2,1)}, u32[]{:S(2)}, u32[]{:S(2)}) async-start(bf16[8,5,4096]{2,1,0:T(8,128)(2,1)} %reshape.358), calls=%async_computation.3 | async-start | bytes 1048576 | tf_op jit(solution)/shard_map/all_to_all | solution.py:126
  464.0 16.1 %all-to-all-done.1 = bf16[8,5,4096]{2,1,0:T(8,128)(2,1)} async-done(((bf16[8,5,4096]{2,1,0:T(8,128)(2,1)}), bf16[8,5,4096]{2,1,0:T(8,128)(2,1)}, u32[]{:S(2)}, u32[]{:S(2)}) %all-to-all-start.1) | async-done | bytes 327712 | tf_op jit(solution)/shard_map/all_to_all | solution.py:126
  480.2 1.2 reshape.366
  481.6 1.7 fusion.64
  (257 shorter events, 29.7 us)
Async XLA Ops:
  7.2 325.2 %copy-start = (bf16[1,384,4096]{2,1,0:T(8,128)(2,1)S(1)}, bf16[1,384,4096]{2,1,0:T(8,128)(2,1)}, u32[]{:S(2)}) copy-start(bf16[1,384,4096]{2,1,0:T(8,128)(2,1)} %param.39) | copy-start | bytes 9437188
  7.2 12.0 %copy-start.2 = (f32[16,1024]{1,0:T(8,128)S(1)}, f32[16,1024]{1,0:T(8,128)}, u32[]{:S(2)}) copy-start(f32[16,1024]{1,0:T(8,128)} %param.28) | copy-start | bytes 196612
  7.2 59.0 %all-gather.11.cloned.1.call-start = ((), (), s32[]{:S(2)}) async-start(), calls=%async_computation.8 | async-start | bytes 2162688 | tf_op jit(solution)/shard_map/all_gather | solution.py:17
  8.1 7.4 %collective-permute-start = (bf16[3,1024]{1,0:T(4,128)(2,1)S(1)}, bf16[3,1024]{1,0:T(4,128)(2,1)S(1)}, u32[]{:S(2)}, u32[]{:S(2)}) collective-permute-start(bf16[3,1024]{1,0:T(4,128)(2,1)S(1)} %slice.264), channel_id=1, source_target_pairs={{0,8},{8,16},{16,24},{24,32},{32,40},{40,48},{48,56},{56,64},{64,7... | collective-permute-start | bytes 18440 | tf_op jit(solution)/shard_map/ppermute | solution.py:12
  13.8 103.8 %all-gather.13.cloned.1.call-start = ((), (), s32[]{:S(2)}) async-start(), calls=%async_computation.9 | async-start | bytes 2162688 | tf_op jit(solution)/shard_map/all_gather | solution.py:17
  16.5 0.8 copy-start.1
  16.5 33.1 %copy-start.12 = (bf16[128,16]{0,1:T(8,128)(2,1)S(1)}, bf16[128,16]{0,1:T(8,128)(2,1)}, u32[]{:S(2)}) copy-start(bf16[128,16]{0,1:T(8,128)(2,1)} %param.27) | copy-start | bytes 12292
  48.1 0.6 copy-start.3
  48.8 135.2 %all-gather.7.cloned.1.call-start = ((), (), s32[]{:S(2)}) async-start(), calls=%async_computation.4 | async-start | bytes 8650752 | tf_op jit(solution)/shard_map/all_gather | solution.py:86
  49.5 187.4 %reduce-scatter.3.cloned.1.call-start = ((), (), s32[]{:S(2)}) async-start(), calls=%async_computation.5 | async-start | bytes 1179648 | tf_op jit(solution)/shard_map/reduce_scatter | solution.py:87
  119.3 44.5 %copy-start.9 = (f32[1024]{0:T(1024)S(1)}, f32[1024]{0:T(1024)}, u32[]{:S(2)}) copy-start(f32[1024]{0:T(1024)} %param.30) | copy-start | bytes 12292
  119.4 44.5 %copy-start.11 = (f32[1024]{0:T(1024)S(1)}, f32[1024]{0:T(1024)}, u32[]{:S(2)}) copy-start(f32[1024]{0:T(1024)} %param.31) | copy-start | bytes 12292
  166.3 23.4 %copy-start.4 = (bf16[128,1024]{1,0:T(8,128)(2,1)}, bf16[128,1024]{1,0:T(8,128)(2,1)S(1)}, u32[]{:S(2)}) copy-start(bf16[128,1024]{1,0:T(8,128)(2,1)S(1)} %fusion.58) | copy-start | bytes 786436
  166.4 70.6 %copy-start.7 = (bf16[16,4096]{1,0:T(8,128)(2,1)S(1)}, bf16[16,4096]{1,0:T(8,128)(2,1)}, u32[]{:S(2)}) copy-start(bf16[16,4096]{1,0:T(8,128)(2,1)} %param.33) | copy-start | bytes 393220
  166.4 71.6 %copy-start.10 = (f32[4096]{0:T(1024)S(1)}, f32[4096]{0:T(1024)}, u32[]{:S(2)}) copy-start(f32[4096]{0:T(1024)} %param.34) | copy-start | bytes 49156
  189.7 132.4 %all-gather.9.cloned.1.call-start = ((), (), s32[]{:S(2)}) async-start(), calls=%async_computation.6 | async-start | bytes 10813440 | tf_op jit(solution)/shard_map/all_gather | solution.py:118
  239.0 0.7 copy-start.5
  262.6 192.2 %reduce-scatter.5.cloned.1.call-start = ((), (), s32[]{:S(2)}) async-start(), calls=%async_computation.7 | async-start | bytes 10813440 | tf_op jit(solution)/shard_map/reduce_scatter | solution.py:123
  349.6 114.2 %copy-start.14 = (s32[32]{0:T(128)S(1)}, s32[32]{0:T(128)}, u32[]{:S(2)}) copy-start(s32[32]{0:T(128)} %multiply_add_fusion.8) | copy-start | bytes 388
  349.6 114.3 %copy-start.6 = (bf16[16,4096]{1,0:T(8,128)(2,1)S(1)}, bf16[16,4096]{1,0:T(8,128)(2,1)}, u32[]{:S(2)}) copy-start(bf16[16,4096]{1,0:T(8,128)(2,1)} %copy-done.5) | copy-start | bytes 393220
  349.6 114.3 %copy-start.8 = (bf16[4096,8]{0,1:T(8,128)(2,1)S(1)}, bf16[4096,8]{0,1:T(8,128)(2,1)}, u32[]{:S(2)}) copy-start(bf16[4096,8]{0,1:T(8,128)(2,1)} %param.35) | copy-start | bytes 196612
  349.6 114.4 %copy-start.13 = (s32[16,2]{0,1:T(2,128)S(1)}, s32[16,2]{0,1:T(2,128)}, u32[]{:S(2)}) copy-start(s32[16,2]{0,1:T(2,128)} %param.36) | copy-start | bytes 388
  456.7 23.4 %all-to-all-start.1 = ((bf16[8,5,4096]{2,1,0:T(8,128)(2,1)}), bf16[8,5,4096]{2,1,0:T(8,128)(2,1)}, u32[]{:S(2)}, u32[]{:S(2)}) async-start(bf16[8,5,4096]{2,1,0:T(8,128)(2,1)} %reshape.358), calls=%async_computation.3 | async-start | bytes 1048576 | tf_op jit(solution)/shard_map/all_to_all | solution.py:126
Sparse Core Ops, SparseCore 0:
  13.9 52.2 all-gather.10
  69.3 48.1 all-gather.12
  120.0 63.9 all-gather.6
  189.9 47.0 reduce-scatter.2
  262.7 59.3 all-gather.8
  349.7 105.0 reduce-scatter.4
where the time goes:
time: 497 us; the launch traced here: 490 us
  waiting for transfers between devices  312 us (63%)
  other arithmetic  76.2 us (15%)
  matrix products  34.6 us (7%)
  local copies, waits for them, and re-layouts  24.2 us (5%)
  blocking collectives  17.9 us (4%)
  between operations  14.4 us (3%)
  starting transfers between devices  9.3 us (2%)
    reduce_scatter x1, waiting for transfers between devices, shards(): lax.psum_scatter(partial_out.astype(jnp.bfloat16), 'seq', scatter_dimensi...  105 us
    all_gather x2, waiting for transfers between devices, carried_in(): gathered = jax.tree.map(lambda a: lax.all_gather(a, axis), part)  67.8 us
    all_gather x1, waiting for transfers between devices, shards(): piece = lax.all_gather(flat_rows, 'seq', axis=0, tiled=True)  59.5 us
    slice x32, other arithmetic, sweep(): lax.scan(advance, state, (delta, convolved, input_rows, output_rows), unr...  50.8 us
    reduce_scatter x1, waiting for transfers between devices, shards(): lax.psum_scatter(jnp.dot(mixed, full_weight, preferred_element_type=jnp.f...  45.4 us
    all_to_all x1, blocking collectives, shards(): lax.all_to_all(outgoing, 'exp', split_axis=0, concat_axis=0, tiled=True)  17.9 us
    all_gather x1, waiting for transfers between devices, shards(): full_weight = lax.all_gather(out_weight, 'seq', axis=1, tiled=True)  17.6 us
    dot_general x1, matrix products, shards(): jnp.dot(activated, down_weight[0], preferred_element_type=jnp.float32)  17.2 us
  transfers between devices with their start and end apart: 8, of which 7 were waited for; matrix products, arithmetic and copies ran while one was open for 18% of the time, Pallas kernels for 0%

commit v1 on v0

--- a/solution.py
+++ b/solution.py
@@ -2,6 +2,7 @@
 import jax.numpy as jnp
 from jax import lax
 from jax.sharding import PartitionSpec as P
+from jax.lax import all_to_all, psum
 
 KCONV = 4
 
@@ -115,7 +116,15 @@
     )
     arrived = lax.all_to_all(outgoing, "exp", split_axis=0, concat_axis=0, tiled=True)
     flat_rows = arrived.reshape(-1, arrived.shape[2])
-    piece = lax.all_gather(flat_rows, "seq", axis=0, tiled=True)
+    piece = jnp.concatenate(
+        all_to_all(
+            jnp.stack([flat_rows] * psum(1, axis_name="seq"), 0),
+            axis_name="seq",
+            split_axis=0,
+            concat_axis=0,
+        ),
+        0,
+    )
     gating = jnp.dot(piece, gate_weight[0], preferred_element_type=jnp.float32)
     upward = jnp.dot(piece, up_weight[0], preferred_element_type=jnp.float32)
     activated = (jax.nn.silu(gating) * upward).astype(jnp.bfloat16)

time: 497 us -> 559 us (1.12)
  blocking collectives: 17.9 us -> 143 us
  waiting for transfers between devices: 312 us -> 254 us
  other arithmetic: 76.2 us -> 68.1 us
  local copies, waits for them, and re-layouts: 24.2 us -> 31.7 us
    all_to_all x0 -> x1, blocking collectives: none -> 125 us  [shards(): all_to_all(jnp.stack([flat_rows] * psum(1, axis_name='seq'), 0), axis_nam...]
    all_gather x1 -> x0, waiting for transfers between devices: 59.5 us -> none  [shards(): piece = lax.all_gather(flat_rows, 'seq', axis=0, tiled=True)]
    slice x32, other arithmetic: 50.8 us -> 43.1 us  [sweep(): lax.scan(advance, state, (delta, convolved, input_rows, output_rows), unr...]
    another operation x0 -> x2, local copies, waits for them, and re-layouts: none -> 6.47 us  [shards(): jnp.stack([flat_rows] * psum(1, axis_name='seq'), 0)]
  transfers between devices with their start and end apart: 8 -> 7, of which waited for: 7 -> 6; matrix products, arithmetic and copies ran while one was open for 18% -> 14% of each run, Pallas kernels for 0% -> 0%
where the time goes in v1:
time: 559 us; the launch traced here: 553 us
  waiting for transfers between devices  254 us (45%)
  blocking collectives  143 us (26%)
  other arithmetic  68.1 us (12%)
  local copies, waits for them, and re-layouts  31.7 us (6%)
  matrix products  31.4 us (6%)
  between operations  14 us (3%)
  starting transfers between devices  9.25 us (2%)
    all_to_all x1, blocking collectives, shards(): all_to_all(jnp.stack([flat_rows] * psum(1, axis_name='seq'), 0), axis_nam...  125 us
    reduce_scatter x1, waiting for transfers between devices, shards(): lax.psum_scatter(partial_out.astype(jnp.bfloat16), 'seq', scatter_dimensi...  101 us
    all_gather x2, waiting for transfers between devices, carried_in(): gathered = jax.tree.map(lambda a: lax.all_gather(a, axis), part)  71.7 us
    slice x32, other arithmetic, sweep(): lax.scan(advance, state, (delta, convolved, input_rows, output_rows), unr...  43.1 us
    reduce_scatter x1, waiting for transfers between devices, shards(): lax.psum_scatter(jnp.dot(mixed, full_weight, preferred_element_type=jnp.f...  42.5 us
    all_gather x1, waiting for transfers between devices, shards(): full_weight = lax.all_gather(out_weight, 'seq', axis=1, tiled=True)  21.6 us
    all_to_all x1, blocking collectives, shards(): lax.all_to_all(outgoing, 'exp', split_axis=0, concat_axis=0, tiled=True)  17.9 us
    dot_general x1, matrix products, shards(): jnp.dot(activated, down_weight[0], preferred_element_type=jnp.float32)  17.3 us
  transfers between devices with their start and end apart: 7, of which 6 were waited for; matrix products, arithmetic and copies ran while one was open for 14% of the time, Pallas kernels for 0%

profile of v1, /device:TPU:2, one launch (start us, length us, event | category | flops | bytes accessed | tf_op | source)
XLA Modules:
  0.0 552.7 jit_solution(16250137498817357403)
XLA Ops:
  8.1 2.0 collective-permute-start
  10.2 2.1 fusion.59
  12.2 1.5 multiply_exponential_fusion
  15.5 1.0 maximum_convert_fusion
  17.4 1.8 fusion.81
  19.2 25.1 %while.37 = (s32[]{:T(128)}, f32[16,1024]{1,0:T(8,128)S(1)}, f32[16,8,1024]{2,1,0:T(8,128)}, f32[16,1024]{1,0:T(8,128)S(1)}, f32[16,8,16]{2,1,0:T(8,128)S(1)}, /...) while((s32[]{:T(128)}, f32[16,1024]{1,0:T(8,128)S(1)}, ...), condition=%wide.region_2.3_spmd.clone, body=%wide.region_1.2_spmd.clone.sunk | while | flops 811018 | bytes 396055 | solution.py:37
  19.2 1.3 constant_dynamic-slice_fusion.41
  20.7 1.6 constant_dynamic-slice_fusion.41
  22.5 1.3 constant_dynamic-slice_fusion.41
  24.0 1.3 constant_dynamic-slice_fusion.41
  25.6 1.3 constant_dynamic-slice_fusion.41
  27.1 1.4 constant_dynamic-slice_fusion.41
  28.7 1.3 constant_dynamic-slice_fusion.41
  30.2 1.3 constant_dynamic-slice_fusion.41
  31.8 1.3 constant_dynamic-slice_fusion.41
  33.3 1.3 constant_dynamic-slice_fusion.41
  34.8 1.5 constant_dynamic-slice_fusion.41
  36.6 1.3 constant_dynamic-slice_fusion.41
  38.1 1.3 constant_dynamic-slice_fusion.41
  39.7 1.3 constant_dynamic-slice_fusion.41
  41.2 1.3 constant_dynamic-slice_fusion.41
  42.8 1.3 constant_dynamic-slice_fusion.41
  45.8 20.4 %all-gather.8.cloned.1.call-done = f32[512,1024]{1,0:T(8,128)} async-done(((f32[16,1024]{1,0:T(8,128)}), f32[512,1024]{1,0:T(8,128)}) %all-gather.8.cloned.1.call-update) | async-done | bytes 2097168 | tf_op jit(solution)/shard_map/all_gather | solution.py:18
  66.2 51.3 %all-gather.10.cloned.1.call-done = f32[512,1024]{1,0:T(8,128)} async-done(((f32[16,1024]{1,0:T(8,128)}), f32[512,1024]{1,0:T(8,128)}) %all-gather.10.cloned.1.call-update) | async-done | bytes 2097168 | tf_op jit(solution)/shard_map/all_gather | solution.py:18
  117.5 1.8 while.35
  118.4 0.9 bitcast_add_fusion.3
  119.4 40.5 %while.36 = (s32[]{:T(128)}, f32[16,1024]{1,0:T(8,128)S(1)}, f32[16,8,1024]{2,1,0:T(8,128)}, f32[16,8,1024]{2,1,0:T(8,128)}, f32[16,1024]{1,0:T(8,128)S(1)}, /*i...) while((s32[]{:T(128)}, f32[16,1024]{1,0:T(8,128)S(1)}, ...), condition=%wide.region_14.15_spmd, body=%wide.region_5.14_spmd.sunk | while | flops 1441801 | bytes 1316385 | solution.py:37
  119.4 1.3 constant_dynamic-slice_fusion.40
  121.9 1.6 constant_dynamic-slice_fusion.40
  124.7 1.3 constant_dynamic-slice_fusion.40
  127.2 1.3 constant_dynamic-slice_fusion.40
  129.6 1.3 constant_dynamic-slice_fusion.40
  132.1 1.4 constant_dynamic-slice_fusion.40
  134.7 1.3 constant_dynamic-slice_fusion.40
  137.2 1.3 constant_dynamic-slice_fusion.40
  139.7 1.3 constant_dynamic-slice_fusion.40
  142.2 1.3 constant_dynamic-slice_fusion.40
  144.7 1.5 constant_dynamic-slice_fusion.40
  147.4 1.3 constant_dynamic-slice_fusion.40
  149.9 1.3 constant_dynamic-slice_fusion.40
  152.4 1.3 constant_dynamic-slice_fusion.40
  154.9 1.3 constant_dynamic-slice_fusion.40
  157.4 1.3 constant_dynamic-slice_fusion.40
  159.9 2.5 fusion.58
  162.4 21.6 %all-gather.6.cloned.1.call-done = bf16[1024,4096]{1,0:T(8,128)(2,1)} async-done(((bf16[1024,128]{1,0:T(8,128)(2,1)}), bf16[1024,4096]{1,0:T(8,128)(2,1)}) %all-gather.6.cloned.1.call-update) | async-done | bytes 8388624 | tf_op jit(solution)/shard_map/all_gather | solution.py:87
  184.0 5.7 %convolution_convert_fusion.1 = bf16[128,4096]{1,0:T(8,128)(2,1)} fusion(bf16[128,1024]{1,0:T(8,128)(2,1)S(1)} %fusion.58, bf16[1024,4096]{1,0:T(8,128)(2,1)} %all-gather.6.cloned.1.call-done), kind=kOutput, calls=%fused_computation.111 | convolution fusion | flops 1074266112 | bytes 9699328 | tf_op jit(solution)/shard_map/dot_general | solution.py:89
  190.3 42.5 %reduce-scatter.3.cloned.1.call-done = bf16[16,4096]{1,0:T(8,128)(2,1)} async-done(((bf16[128,4096]{1,0:T(8,128)(2,1)}), bf16[16,4096]{1,0:T(8,128)(2,1)}) %reduce-scatter.3.cloned.1.call-update) | async-done | bytes 131088 | tf_op jit(solution)/shard_map/reduce_scatter | solution.py:88
  232.8 1.1 multiply_reduce_fusion.8
  234.0 1.1 multiply_convert_fusion
  236.7 1.2 convolution_convert_fusion.2
  237.9 0.9 reshape.358
  238.8 17.9 %all_to_all.15 = bf16[8,5,4096]{2,1,0:T(8,128)(2,1)} all-to-all(bf16[8,5,4096]{2,1,0:T(8,128)(2,1)} %reshape.358), channel_id=1, replica_groups=mesh['seq'=32,'exp'=8] {'exp'}, dimensions={0} | all-to-all | bytes 655360 | tf_op jit(solution)/shard_map/all_to_all | solution.py:117
  256.7 1.2 stack_reshape.2
  257.9 5.3 stack.3
  263.2 124.9 %all_to_all.16 = bf16[32,40,4096]{2,1,0:T(8,128)(2,1)S(1)} all-to-all(bf16[32,40,4096]{2,1,0:T(8,128)(2,1)} %stack.3), channel_id=1, replica_groups=mesh['seq'=32,'exp'=8] {'seq'}, dimensions={0} | all-to-all | bytes 20971520 | tf_op jit(solution)/shard_map/all_to_all | solution.py:120
  388.1 3.8 copy-done.3
  391.9 6.9 %fusion.33 = f32[1280,384]{1,0:T(8,128)} fusion(bf16[1280,4096]{1,0:T(8,128)(2,1)S(1)} %bitcast.247, bf16[1,4096,384]{2,1,0:T(8,128)(2,1)S(1)} %copy-done.14), kind=kOutput, calls=%fused_computation.116 | convolution fusion | flops 4026531840 | bytes 15597568 | tf_op jit(solution)/shard_map/dot_general | solution.py:128
  398.8 17.3 %convolution_convert_fusion = bf16[1280,4096]{1,0:T(8,128)(2,1)} fusion(bf16[1,384,4096]{2,1,0:T(8,128)(2,1)S(1)} %copy-done, bf16[1280,4096]{1,0:T(8,128)(2,1)} %bitcast.248, bf16[1,4096,384]{2,1,0:T(8,128)(2,1)} %param.38, f32[1280,384]{1,0:T(8,128)} %fusion.33), kind=kOutput, calls=%fused_computation.110 | convolution fusion | flops 8061255680 | bytes 29229056 | tf_op jit(solution)/shard_map/dot_general | solution.py:131
  416.1 101.5 %reduce-scatter.5.cloned.1.call-done = bf16[40,4096]{1,0:T(8,128)(2,1)} async-done(((bf16[1280,4096]{1,0:T(8,128)(2,1)}), bf16[40,4096]{1,0:T(8,128)(2,1)}) %reduce-scatter.5.cloned.1.call-update) | async-done | bytes 327696 | tf_op jit(solution)/shard_map/reduce_scatter | solution.py:132
  517.6 1.9 reshape.360
  519.5 7.0 %all-to-all-start.2 = ((bf16[8,5,4096]{2,1,0:T(8,128)(2,1)}), bf16[8,5,4096]{2,1,0:T(8,128)(2,1)}, u32[]{:S(2)}, u32[]{:S(2)}) async-start(bf16[8,5,4096]{2,1,0:T(8,128)(2,1)} %reshape.360), calls=%async_computation.4 | async-start | bytes 1048576 | tf_op jit(solution)/shard_map/all_to_all | solution.py:135
  526.8 16.2 %all-to-all-done.2 = bf16[8,5,4096]{2,1,0:T(8,128)(2,1)} async-done(((bf16[8,5,4096]{2,1,0:T(8,128)(2,1)}), bf16[8,5,4096]{2,1,0:T(8,128)(2,1)}, u32[]{:S(2)}, u32[]{:S(2)}) %all-to-all-start.2) | async-done | bytes 327712 | tf_op jit(solution)/shard_map/all_to_all | solution.py:135
  543.0 1.2 reshape.368
  544.4 1.7 fusion.64
  (256 shorter events, 30.0 us)
Async XLA Ops:
  7.2 391.7 %copy-start = (bf16[1,384,4096]{2,1,0:T(8,128)(2,1)S(1)}, bf16[1,384,4096]{2,1,0:T(8,128)(2,1)}, u32[]{:S(2)}) copy-start(bf16[1,384,4096]{2,1,0:T(8,128)(2,1)} %param.39) | copy-start | bytes 9437188
  7.2 12.0 %copy-start.2 = (f32[16,1024]{1,0:T(8,128)S(1)}, f32[16,1024]{1,0:T(8,128)}, u32[]{:S(2)}) copy-start(f32[16,1024]{1,0:T(8,128)} %param.28) | copy-start | bytes 196612
  7.2 59.0 %all-gather.8.cloned.1.call-start = ((), (), s32[]{:S(2)}) async-start(), calls=%async_computation.8 | async-start | bytes 2162688 | tf_op jit(solution)/shard_map/all_gather | solution.py:18
  8.1 7.4 %collective-permute-start = (bf16[3,1024]{1,0:T(4,128)(2,1)S(1)}, bf16[3,1024]{1,0:T(4,128)(2,1)S(1)}, u32[]{:S(2)}, u32[]{:S(2)}) collective-permute-start(bf16[3,1024]{1,0:T(4,128)(2,1)S(1)} %slice.264), channel_id=1, source_target_pairs={{0,8},{8,16},{16,24},{24,32},{32,40},{40,48},{48,56},{56,64},{64,7... | collective-permute-start | bytes 18440 | tf_op jit(solution)/shard_map/ppermute | solution.py:13
  13.8 103.8 %all-gather.10.cloned.1.call-start = ((), (), s32[]{:S(2)}) async-start(), calls=%async_computation.9 | async-start | bytes 2162688 | tf_op jit(solution)/shard_map/all_gather | solution.py:18
  16.5 0.8 copy-start.1
  16.5 29.2 %copy-start.12 = (bf16[128,16]{0,1:T(8,128)(2,1)S(1)}, bf16[128,16]{0,1:T(8,128)(2,1)}, u32[]{:S(2)}) copy-start(bf16[128,16]{0,1:T(8,128)(2,1)} %param.27) | copy-start | bytes 12292
  44.3 0.6 copy-start.4
  44.9 139.1 %all-gather.6.cloned.1.call-start = ((), (), s32[]{:S(2)}) async-start(), calls=%async_computation.5 | async-start | bytes 8650752 | tf_op jit(solution)/shard_map/all_gather | solution.py:87
  45.7 187.2 %reduce-scatter.3.cloned.1.call-start = ((), (), s32[]{:S(2)}) async-start(), calls=%async_computation.6 | async-start | bytes 1179648 | tf_op jit(solution)/shard_map/reduce_scatter | solution.py:88
  119.4 40.5 %copy-start.9 = (f32[1024]{0:T(1024)S(1)}, f32[1024]{0:T(1024)}, u32[]{:S(2)}) copy-start(f32[1024]{0:T(1024)} %param.30) | copy-start | bytes 12292
  119.4 40.5 %copy-start.11 = (f32[1024]{0:T(1024)S(1)}, f32[1024]{0:T(1024)}, u32[]{:S(2)}) copy-start(f32[1024]{0:T(1024)} %param.31) | copy-start | bytes 12292
  162.4 27.3 %copy-start.5 = (bf16[128,1024]{1,0:T(8,128)(2,1)}, bf16[128,1024]{1,0:T(8,128)(2,1)S(1)}, u32[]{:S(2)}) copy-start(bf16[128,1024]{1,0:T(8,128)(2,1)S(1)} %fusion.58) | copy-start | bytes 786436
  162.4 27.4 %copy-start.13 = (s32[16,2]{0,1:T(2,128)S(1)}, s32[16,2]{0,1:T(2,128)}, u32[]{:S(2)}) copy-start(s32[16,2]{0,1:T(2,128)} %param.36) | copy-start | bytes 388
  162.4 71.5 %copy-start.10 = (f32[4096]{0:T(1024)S(1)}, f32[4096]{0:T(1024)}, u32[]{:S(2)}) copy-start(f32[4096]{0:T(1024)} %param.34) | copy-start | bytes 49156
  189.7 327.9 %reduce-scatter.5.cloned.1.call-start = ((), (), s32[]{:S(2)}) async-start(), calls=%async_computation.7 | async-start | bytes 10813440 | tf_op jit(solution)/shard_map/reduce_scatter | solution.py:132
  235.0 0.7 copy-start.6
  263.2 128.8 %copy-start.14 = (bf16[1,4096,384]{2,1,0:T(8,128)(2,1)S(1)}, bf16[1,4096,384]{2,1,0:T(8,128)(2,1)}, u32[]{:S(2)}) copy-start(bf16[1,4096,384]{2,1,0:T(8,128)(2,1)} %param.37) | copy-start | bytes 9437188
  388.1 3.8 copy-start.3
  416.1 110.5 %copy-start.7 = (bf16[16,4096]{1,0:T(8,128)(2,1)S(1)}, bf16[16,4096]{1,0:T(8,128)(2,1)}, u32[]{:S(2)}) copy-start(bf16[16,4096]{1,0:T(8,128)(2,1)} %copy-done.6) | copy-start | bytes 393220
  416.1 110.5 %copy-start.8 = (bf16[4096,8]{0,1:T(8,128)(2,1)S(1)}, bf16[4096,8]{0,1:T(8,128)(2,1)}, u32[]{:S(2)}) copy-start(bf16[4096,8]{0,1:T(8,128)(2,1)} %param.35) | copy-start | bytes 196612
  519.5 23.5 %all-to-all-start.2 = ((bf16[8,5,4096]{2,1,0:T(8,128)(2,1)}), bf16[8,5,4096]{2,1,0:T(8,128)(2,1)}, u32[]{:S(2)}, u32[]{:S(2)}) async-start(bf16[8,5,4096]{2,1,0:T(8,128)(2,1)} %reshape.360), calls=%async_computation.4 | async-start | bytes 1048576 | tf_op jit(solution)/shard_map/all_to_all | solution.py:135
Sparse Core Ops, SparseCore 0:
  13.9 52.2 all-gather.7
  69.3 48.1 all-gather.9
  120.0 63.9 all-gather.5
  189.8 42.9 reduce-scatter.2
  416.3 101.2 reduce-scatter.4
